TPU v7x, 256 devices: a whole 4x4x8 slice. The times are simulated.
256 devices in a mesh: blk: 8 (over y_lo, x), tile: 32 (over y_hi, z, core).
Axes of the slice: x: 4, y: 4 (y_hi: 2, y_lo: 2; y = y_hi * 2 + y_lo), z: 8, core: 2. Of those that a mesh axis runs over, the one named last changes fastest.
Arguments:
- qkv: bfloat16 [3, 8192, 4096], P(None, ('blk', 'tile')), may hold values from -33 to 33
- frame_clip: int32 [16], replicated, may hold values from 0 to 2, never falling along the last dimension, each value on 1 to 10 neighbouring positions
- w_out: bfloat16 [4096, 5120], P('tile'), may hold values from -0.5 to 0.5
Outputs:
- projected: bfloat16 [8192, 5120], P(('blk', 'tile'))
All inputs are finite; a program needn't handle non-finite values.
Results may differ from a plain program's by a relative error of at most 0.023.
Values may be sent and summed in bfloat16 or wider, within the bound.
A program may use at most 64 MiB of HBM per device.

v0:
```python
import math
import jax
import jax.numpy as jnp
from jax import lax
from jax.sharding import PartitionSpec as P

FRB = 2
TPF = 16


def clip_lookup(frames, frame_clip):
    table = jnp.arange(frame_clip.shape[0], dtype=jnp.int32)
    hits = (frames[..., None] == table).astype(jnp.int32)
    return jnp.sum(hits * frame_clip, axis=-1)


def on_device(qkv, frame_clip, w_out):
    tiles = lax.axis_size("tile")
    blk_index = lax.axis_index("blk")
    tok_dev = qkv.shape[1]
    head_dim = w_out.shape[0]
    tok_blk = tok_dev * tiles
    scale = 1.0 / math.sqrt(head_dim)
    local = lax.all_to_all(qkv, "tile", split_axis=2, concat_axis=1, tiled=True)
    queries = local[0]
    keys_all = local[1]
    values_all = local[2]
    rows = jnp.arange(tok_blk, dtype=jnp.int32)
    query_clip = clip_lookup(blk_index * FRB + rows % tok_dev // TPF, frame_clip)
    start_state = (
        jnp.full((tok_blk,), -1e30, jnp.float32),
        jnp.zeros((tok_blk,), jnp.float32),
        jnp.zeros((tok_blk, head_dim), jnp.float32),
    )
    carry = start_state
    key_piece = lax.all_gather(keys_all, "blk", axis=0, tiled=True)
    value_piece = lax.all_gather(values_all, "blk", axis=0, tiled=True)
    count = key_piece.shape[0]
    width = math.gcd(count, tok_blk)
    key_blocks = key_piece.reshape(count // width, width, head_dim)
    value_blocks = value_piece.reshape(count // width, width, head_dim)
    firsts = width * jnp.arange(count // width, dtype=jnp.int32)

    def advance(state, item):
        key_block, value_block, first = item
        index = first + jnp.arange(width, dtype=jnp.int32)
        key_clip = clip_lookup(index // tok_blk * FRB + index % tok_dev // TPF, frame_clip)
        allowed = query_clip[:, None] == key_clip[None, :]
        run_max, run_sum, run_acc = state
        scores = (
            jnp.einsum("qd,kd->qk", queries, key_block, preferred_element_type=jnp.float32) * scale
        )
        masked = jnp.where(allowed, scores, -1e30)
        new_max = jnp.maximum(run_max, jnp.max(masked, axis=1))
        weights = jnp.where(allowed, jnp.exp(scores - new_max[:, None]), 0.0)
        factor = jnp.exp(run_max - new_max)
        new_sum = run_sum * factor + jnp.sum(weights, axis=1)
        new_acc = run_acc * factor[:, None] + jnp.dot(
            weights.astype(jnp.bfloat16), value_block, preferred_element_type=jnp.float32
        )
        state = (new_max, new_sum, new_acc)
        return (state, None)

    carry, unused = lax.scan(advance, carry, (key_blocks, value_blocks, firsts))
    run_max, run_sum, run_acc = carry
    attn = (run_acc / run_sum[:, None]).astype(jnp.bfloat16)
    return lax.psum_scatter(
        jnp.dot(attn, w_out, preferred_element_type=jnp.float32).astype(jnp.bfloat16),
        "tile",
        scatter_dimension=0,
        tiled=True,
    )


def solution(mesh):
    in_specs = (P(None, ("blk", "tile"), None), P(), P("tile", None))
    out_specs = P(("blk", "tile"), None)
    return jax.shard_map(
        on_device, mesh=mesh, in_specs=in_specs, out_specs=out_specs, check_vma=False
    )
```

profile of v0, /device:TPU:2, one launch (start us, length us, event | category | flops | bytes accessed | tf_op | source)
XLA Modules:
  0.0 374.8 jit_solution(4900958124774167915)
XLA Ops:
  6.5 6.1 %copy.17 = bf16[3,32,4096]{1,0,2:T(4,128)(2,1)} copy(bf16[3,32,4096]{2,1,0:T(8,128)(2,1)} %param.5) | data formatting | bytes 1572864 | tf_op args[0]
  12.6 6.2 %reshape.88 = bf16[32,2,6144]{2,1,0:T(2,128)(2,1)S(1)} reshape(bf16[4096,3,32]{2,1,0:T(4,128)(2,1)} %bitcast.49) | data formatting | bytes 1572864
  18.8 36.1 %all_to_all.15 = bf16[32,2,6144]{2,1,0:T(2,128)(2,1)S(1)} all-to-all(bf16[32,2,6144]{2,1,0:T(2,128)(2,1)S(1)} %reshape.88), channel_id=1, replica_groups=mesh['blk'=8,'tile'=32] {'tile'}, dimensions={0} | all-to-all | bytes 1572864 | tf_op jit(solution)/shard_map/all_to_all | solution.py:24
  55.0 4.9 %reshape.89 = bf16[4096,3,32]{2,1,0:T(4,128)(2,1)} reshape(bf16[32,2,6144]{2,1,0:T(2,128)(2,1)S(1)} %all_to_all.15) | data formatting | bytes 1572864
  59.8 4.2 %copy.22 = bf16[3,32,32,128]{3,2,1,0:T(8,128)(2,1)S(1)} copy(bf16[3,32,32,128]{1,0,3,2:T(4,128)(2,1)} %bitcast.48) | data formatting | bytes 1572864 | tf_op jit(solution)/shard_map/all_to_all | solution.py:24
  66.2 35.8 %all-gather.5.cloned.1.call-done = bf16[8192,128]{1,0:T(8,128)(2,1)} async-done(((bf16[1024,128]{1,0:T(8,128)(2,1)}), bf16[8192,128]{1,0:T(8,128)(2,1)}) %all-gather.5.cloned.1.call-update) | async-done | bytes 2097168 | tf_op jit(solution)/shard_map/all_gather | solution.py:37
  101.9 45.2 %all-gather.3.cloned.1.call-done = bf16[8192,128]{1,0:T(8,128)(2,1)} async-done(((bf16[1024,128]{1,0:T(8,128)(2,1)}), bf16[8192,128]{1,0:T(8,128)(2,1)}) %all-gather.3.cloned.1.call-update) | async-done | bytes 2097168 | tf_op jit(solution)/shard_map/all_gather | solution.py:36
  147.1 50.5 %while.18 = (s32[]{:T(128)}, f32[1024]{0:T(1024)S(1)}, f32[1024]{0:T(1024)S(1)}, f32[1024,128]{1,0:T(8,128)S(1)}, s32[1024]{0:T(1024)S(1)}, /*index=5*/s32[8]{0:...) while((s32[]{:T(128)}, f32[1024]{0:T(1024)S(1)}, ...), condition=%wide.region_5.6_spmd.clone, body=%wide.region_1.5_spmd.clone.sunk | while | flops 552039424 | bytes 14520545 | solution.py:64
  148.4 1.7 fusion.53
  150.2 1.0 fusion.54
  151.2 2.2 fusion.56
  154.8 1.7 fusion.53
  156.5 1.0 fusion.54
  157.5 2.2 fusion.56
  161.1 1.7 fusion.53
  162.8 1.0 fusion.54
  163.8 2.2 fusion.56
  167.4 1.7 fusion.53
  169.1 1.0 fusion.54
  170.1 2.2 fusion.56
  173.7 1.7 fusion.53
  175.4 1.0 fusion.54
  176.4 2.2 fusion.56
  180.0 1.7 fusion.53
  181.7 1.0 fusion.54
  182.7 2.2 fusion.56
  186.3 1.7 fusion.53
  189.0 2.2 fusion.56
  192.6 1.7 fusion.53
  195.3 2.2 fusion.56
  197.6 5.6 %convolution_convert_fusion = bf16[1024,5120]{1,0:T(8,128)(2,1)} fusion(bf16[128,5120]{1,0:T(8,128)(2,1)S(1)} %copy-done, f32[1024,128]{1,0:T(8,128)S(1)} %get-tuple-element.169, f32[1024]{0:T(1024)S(1)} %get-tuple-element.170), kind=kOutput, calls=%fused_computation.49 | convolution fusion | flops 1347682304 | bytes 12324864 | tf_op jit(solution)/shard_map/dot_general | solution.py:68
  203.2 165.0 %reduce-scatter.2.cloned.1.call-done = bf16[32,5120]{1,0:T(8,128)(2,1)} async-done(((bf16[1024,5120]{1,0:T(8,128)(2,1)}), bf16[32,5120]{1,0:T(8,128)(2,1)}) %reduce-scatter.2.cloned.1.call-update) | async-done | bytes 327696 | tf_op jit(solution)/shard_map/reduce_scatter | solution.py:67
  (70 shorter events, 14.8 us)
Async XLA Ops:
  6.5 191.0 %copy-start = (bf16[128,5120]{1,0:T(8,128)(2,1)S(1)}, bf16[128,5120]{1,0:T(8,128)(2,1)}, u32[]{:S(2)}) copy-start(bf16[128,5120]{1,0:T(8,128)(2,1)} %param.7) | copy-start | bytes 3932164
  6.5 95.4 %all-gather.5.cloned.1.call-start = ((), (), s32[]{:S(2)}) async-start(), calls=%async_computation.3 | async-start | bytes 2359296 | tf_op jit(solution)/shard_map/all_gather | solution.py:37
  59.8 6.1 %copy-start.1 = (s32[16]{0:T(128)S(1)}, s32[16]{0:T(128)}, u32[]{:S(2)}) copy-start(s32[16]{0:T(128)} %param.6) | copy-start | bytes 196
  64.9 82.2 %all-gather.3.cloned.1.call-start = ((), (), s32[]{:S(2)}) async-start(), calls=%async_computation.2 | async-start | bytes 2359296 | tf_op jit(solution)/shard_map/all_gather | solution.py:36
  65.8 302.4 %reduce-scatter.2.cloned.1.call-start = ((), (), s32[]{:S(2)}) async-start(), calls=%async_computation.4 | async-start | bytes 10813440 | tf_op jit(solution)/shard_map/reduce_scatter | solution.py:67
Sparse Core Ops, SparseCore 0:
  65.1 36.8 all-gather.4
  103.7 43.3 all-gather.2
  203.3 164.8 reduce-scatter.1
where the time goes:
time: 376 us; the launch traced here: 375 us
  waiting for transfers between devices  246 us (65%)
  matrix products  37 us (10%)
  blocking collectives  36.1 us (10%)
  local copies, waits for them, and re-layouts  27.9 us (7%)
  other arithmetic  14 us (4%)
  between operations  13.2 us (4%)
    reduce_scatter x1, waiting for transfers between devices, on_device(): lax.psum_scatter(jnp.dot(attn, w_out, preferred_element_type=jnp.float32)...  165 us
    all_gather x1, waiting for transfers between devices, on_device(): key_piece = lax.all_gather(keys_all, 'blk', axis=0, tiled=True)  45.2 us
    all_to_all x1, blocking collectives, on_device(): local = lax.all_to_all(qkv, 'tile', split_axis=2, concat_axis=1, tiled=True)  36.1 us
    all_gather x1, waiting for transfers between devices, on_device(): value_piece = lax.all_gather(values_all, 'blk', axis=0, tiled=True)  35.8 us
    dot_general x8, matrix products, advance(): jnp.dot(weights.astype(jnp.bfloat16), value_block, preferred_element_type...  17.7 us
    unnamed x7, local copies, waits for them, and re-layouts  17.2 us
    dot_general x8, matrix products, advance(): jnp.einsum('qd,kd->qk', queries, key_block, preferred_element_type=jnp.fl...  13.6 us
    reduce_sum x8, other arithmetic, advance(): new_sum = run_sum * factor + jnp.sum(weights, axis=1)  7.79 us
  transfers between devices with their start and end apart: 3, of which 3 were waited for; matrix products, arithmetic and copies ran while one was open for 0% of the time, Pallas kernels for 0%

commit v1 on v0

--- a/solution.py
+++ b/solution.py
@@ -33,8 +33,11 @@
         jnp.zeros((tok_blk, head_dim), jnp.float32),
     )
     carry = start_state
-    key_piece = lax.all_gather(keys_all, "blk", axis=0, tiled=True)
-    value_piece = lax.all_gather(values_all, "blk", axis=0, tiled=True)
+    key_piece, value_piece = jnp.split(
+        lax.all_gather(jnp.concatenate([keys_all, values_all], axis=1), "blk", axis=0, tiled=True),
+        [keys_all.shape[1]],
+        axis=1,
+    )
     count = key_piece.shape[0]
     width = math.gcd(count, tok_blk)
     key_blocks = key_piece.reshape(count // width, width, head_dim)

time: 376 us -> 349 us (0.928)
  waiting for transfers between devices: 246 us -> 212 us
  local copies, waits for them, and re-layouts: 27.9 us -> 38 us
    all_gather x2 -> x1, waiting for transfers between devices: 80.9 us -> 47.2 us  [on_device(): lax.all_gather(jnp.concatenate([keys_all, values_all], axis=1), 'blk', ax...]
    while x8 -> x40, local copies, waits for them, and re-layouts: 0.02 us -> 6.53 us
    dot_general x8, matrix products: 17.7 us -> 12 us  [advance(): jnp.dot(weights.astype(jnp.bfloat16), value_block, preferred_element_type...]
    split x0 -> x1, local copies, waits for them, and re-layouts: none -> 3.82 us  [on_device(): jnp.split(lax.all_gather(jnp.concatenate([keys_all, values_all], axis=1),...]
  transfers between devices with their start and end apart: 3 -> 2, of which waited for: 3 -> 2; matrix products, arithmetic and copies ran while one was open for 0% -> 0% of each run, Pallas kernels for 0% -> 0%
where the time goes in v1:
time: 349 us; the launch traced here: 348 us
  waiting for transfers between devices  212 us (61%)
  local copies, waits for them, and re-layouts  38 us (11%)
  blocking collectives  36.1 us (10%)
  matrix products  33.3 us (10%)
  other arithmetic  14.8 us (4%)
  between operations  13.5 us (4%)
    reduce_scatter x1, waiting for transfers between devices, on_device(): lax.psum_scatter(jnp.dot(attn, w_out, preferred_element_type=jnp.float32)...  165 us
    all_gather x1, waiting for transfers between devices, on_device(): lax.all_gather(jnp.concatenate([keys_all, values_all], axis=1), 'blk', ax...  47.2 us
    all_to_all x1, blocking collectives, on_device(): local = lax.all_to_all(qkv, 'tile', split_axis=2, concat_axis=1, tiled=True)  36.1 us
    unnamed x7, local copies, waits for them, and re-layouts  17.2 us
    dot_general x8, matrix products, advance(): jnp.einsum('qd,kd->qk', queries, key_block, preferred_element_type=jnp.fl...  14.7 us
    dot_general x8, matrix products, advance(): jnp.dot(weights.astype(jnp.bfloat16), value_block, preferred_element_type...  12 us
    reduce_sum x8, other arithmetic, advance(): new_sum = run_sum * factor + jnp.sum(weights, axis=1)  7.81 us
  transfers between devices with their start and end apart: 2, of which 2 were waited for; matrix products, arithmetic and copies ran while one was open for 0% of the time, Pallas kernels for 0%

profile of v1, /device:TPU:2, one launch (start us, length us, event | category | flops | bytes accessed | tf_op | source)
XLA Modules:
  0.0 348.0 jit_solution(6897579178553892683)
XLA Ops:
  6.5 6.1 %copy.17 = bf16[3,32,4096]{1,0,2:T(4,128)(2,1)} copy(bf16[3,32,4096]{2,1,0:T(8,128)(2,1)} %param.5) | data formatting | bytes 1572864 | tf_op args[0]
  12.6 6.2 %reshape.88 = bf16[32,2,6144]{2,1,0:T(2,128)(2,1)S(1)} reshape(bf16[4096,3,32]{2,1,0:T(4,128)(2,1)} %bitcast.49) | data formatting | bytes 1572864
  18.8 36.1 %all_to_all.15 = bf16[32,2,6144]{2,1,0:T(2,128)(2,1)S(1)} all-to-all(bf16[32,2,6144]{2,1,0:T(2,128)(2,1)S(1)} %reshape.88), channel_id=1, replica_groups=mesh['blk'=8,'tile'=32] {'tile'}, dimensions={0} | all-to-all | bytes 1572864 | tf_op jit(solution)/shard_map/all_to_all | solution.py:24
  55.0 4.9 %reshape.89 = bf16[4096,3,32]{2,1,0:T(4,128)(2,1)} reshape(bf16[32,2,6144]{2,1,0:T(2,128)(2,1)S(1)} %all_to_all.15) | data formatting | bytes 1572864
  59.8 4.2 %copy.22 = bf16[3,32,32,128]{3,2,1,0:T(8,128)(2,1)S(1)} copy(bf16[3,32,32,128]{1,0,3,2:T(4,128)(2,1)} %bitcast.48) | data formatting | bytes 1572864 | tf_op jit(solution)/shard_map/all_to_all | solution.py:24
  66.2 47.2 %all-gather.2.cloned.1.call-done = bf16[8192,256]{1,0:T(8,128)(2,1)} async-done(((bf16[1024,256]{1,0:T(8,128)(2,1)}), bf16[8192,256]{1,0:T(8,128)(2,1)}) %all-gather.2.cloned.1.call-update) | async-done | bytes 4194320 | tf_op jit(solution)/shard_map/all_gather | solution.py:37
  113.4 3.8 %fusion.38 = (bf16[8192,128]{1,0:T(8,128)(2,1)S(1)}, bf16[8192,128]{1,0:T(8,128)(2,1)}) fusion(bf16[8192,256]{1,0:T(8,128)(2,1)} %all-gather.2.cloned.1.call-done), kind=kLoop, calls=%fused_computation.70 | loop fusion | bytes 8388608 | tf_op jit(solution)/shard_map/split | solution.py:36
  117.2 52.7 %while.18 = (s32[]{:T(128)}, f32[1024]{0:T(1024)S(1)}, f32[1024]{0:T(1024)S(1)}, f32[1024,128]{1,0:T(8,128)}, s32[1024]{0:T(1024)S(1)}, /*index=5*/s32[8]{0:T(12...) while((s32[]{:T(128)}, f32[1024]{0:T(1024)S(1)}, ...), condition=%wide.region_5.6_spmd.clone, body=%wide.region_1.5_spmd.clone.sunk | while | flops 552039424 | bytes 18714904 | solution.py:67
  118.6 1.8 fusion.54
  120.5 1.0 fusion.55
  121.5 1.5 fusion.57
  125.2 1.8 fusion.54
  127.1 1.0 fusion.55
  128.1 1.5 fusion.57
  131.8 1.8 fusion.54
  133.7 1.0 fusion.55
  134.7 1.5 fusion.57
  138.4 1.8 fusion.54
  140.2 1.0 fusion.55
  141.3 1.5 fusion.57
  145.0 1.8 fusion.54
  146.8 1.0 fusion.55
  147.8 1.5 fusion.57
  151.6 1.8 fusion.54
  153.4 1.0 fusion.55
  154.4 1.5 fusion.57
  158.2 1.8 fusion.54
  161.0 1.5 fusion.57
  164.7 1.8 fusion.54
  167.6 1.5 fusion.57
  169.9 6.6 %convolution_convert_fusion = bf16[1024,5120]{1,0:T(8,128)(2,1)} fusion(bf16[128,5120]{1,0:T(8,128)(2,1)S(1)} %copy-done, f32[1024,128]{1,0:T(8,128)} %get-tuple-element.169, f32[1024]{0:T(1024)S(1)} %get-tuple-element.170), kind=kOutput, calls=%fused_computation.49 | convolution fusion | flops 1347682304 | bytes 12324864 | tf_op jit(solution)/shard_map/dot_general | solution.py:71
  176.6 164.6 %reduce-scatter.2.cloned.1.call-done = bf16[32,5120]{1,0:T(8,128)(2,1)} async-done(((bf16[1024,5120]{1,0:T(8,128)(2,1)}), bf16[32,5120]{1,0:T(8,128)(2,1)}) %reduce-scatter.2.cloned.1.call-update) | async-done | bytes 327696 | tf_op jit(solution)/shard_map/reduce_scatter | solution.py:70
  (101 shorter events, 21.7 us)
Async XLA Ops:
  6.5 163.4 %copy-start = (bf16[128,5120]{1,0:T(8,128)(2,1)S(1)}, bf16[128,5120]{1,0:T(8,128)(2,1)}, u32[]{:S(2)}) copy-start(bf16[128,5120]{1,0:T(8,128)(2,1)} %param.7) | copy-start | bytes 3932164
  6.5 106.9 %all-gather.2.cloned.1.call-start = ((), (), s32[]{:S(2)}) async-start(), calls=%async_computation.2 | async-start | bytes 4718592 | tf_op jit(solution)/shard_map/all_gather | solution.py:37
  59.8 5.5 %copy-start.3 = (s32[16]{0:T(128)S(1)}, s32[16]{0:T(128)}, u32[]{:S(2)}) copy-start(s32[16]{0:T(128)} %param.6) | copy-start | bytes 196
  65.2 275.9 %reduce-scatter.2.cloned.1.call-start = ((), (), s32[]{:S(2)}) async-start(), calls=%async_computation.3 | async-start | bytes 10813440 | tf_op jit(solution)/shard_map/reduce_scatter | solution.py:70
  118.6 2.9 copy-start.1
  123.0 0.8 copy-start.2
  125.2 2.9 copy-start.1
  129.6 0.8 copy-start.2
  131.8 2.9 copy-start.1
  136.2 0.8 copy-start.2
  138.4 2.9 copy-start.1
  142.8 0.8 copy-start.2
  145.0 2.9 copy-start.1
  149.3 0.8 copy-start.2
  151.6 2.9 copy-start.1
  155.9 0.8 copy-start.2
  158.1 2.9 copy-start.1
  162.5 0.8 copy-start.2
  164.7 2.9 copy-start.1
  169.1 0.8 copy-start.2
Sparse Core Ops, SparseCore 0:
  65.3 48.0 all-gather.1
  176.7 164.4 reduce-scatter.1

commit v2 on v0

--- a/solution.py
+++ b/solution.py
@@ -33,7 +33,9 @@
         jnp.zeros((tok_blk, head_dim), jnp.float32),
     )
     carry = start_state
-    key_piece = lax.all_gather(keys_all, "blk", axis=0, tiled=True)
+    key_piece = jnp.concatenate(
+        lax.all_to_all(jnp.stack([keys_all] * lax.axis_size("blk")), "blk", 0, 0), axis=0
+    )
     value_piece = lax.all_gather(values_all, "blk", axis=0, tiled=True)
     count = key_piece.shape[0]
     width = math.gcd(count, tok_blk)

time: 376 us -> 361 us (0.960)
  waiting for transfers between devices: 246 us -> 214 us
  local copies, waits for them, and re-layouts: 27.9 us -> 37.4 us
  starting transfers between devices: 0.09 us -> 4.95 us
    all_gather x1 -> x0, waiting for transfers between devices: 45.2 us -> none  [on_device(): key_piece = lax.all_gather(keys_all, 'blk', axis=0, tiled=True)]
    all_to_all x0 -> x1, waiting for transfers between devices: none -> 30.8 us  [on_device(): lax.all_to_all(jnp.stack([keys_all] * lax.axis_size('blk')), 'blk', 0, 0)]
    all_gather x1, waiting for transfers between devices: 35.8 us -> 19.4 us  [on_device(): value_piece = lax.all_gather(values_all, 'blk', axis=0, tiled=True)]
    while x8 -> x40, local copies, waits for them, and re-layouts: 0.02 us -> 6.45 us
    all_to_all x0 -> x1, starting transfers between devices: none -> 4.94 us  [on_device(): lax.all_to_all(jnp.stack([keys_all] * lax.axis_size('blk')), 'blk', 0, 0)]
  transfers between devices with their start and end apart: 3 -> 3, of which waited for: 3 -> 3; matrix products, arithmetic and copies ran while one was open for 0% -> 1% of each run, Pallas kernels for 0% -> 0%
where the time goes in v2:
time: 361 us; the launch traced here: 360 us
  waiting for transfers between devices  214 us (59%)
  matrix products  39 us (11%)
  local copies, waits for them, and re-layouts  37.4 us (10%)
  blocking collectives  36.1 us (10%)
  other arithmetic  14 us (4%)
  between operations  13.5 us (4%)
  starting transfers between devices  4.95 us (1%)
    reduce_scatter x1, waiting for transfers between devices, on_device(): lax.psum_scatter(jnp.dot(attn, w_out, preferred_element_type=jnp.float32)...  164 us
    all_to_all x1, blocking collectives, on_device(): local = lax.all_to_all(qkv, 'tile', split_axis=2, concat_axis=1, tiled=True)  36.1 us
    all_to_all x1, waiting for transfers between devices, on_device(): lax.all_to_all(jnp.stack([keys_all] * lax.axis_size('blk')), 'blk', 0, 0)  30.8 us
    all_gather x1, waiting for transfers between devices, on_device(): value_piece = lax.all_gather(values_all, 'blk', axis=0, tiled=True)  19.4 us
    dot_general x8, matrix products, advance(): jnp.dot(weights.astype(jnp.bfloat16), value_block, preferred_element_type...  18.4 us
    unnamed x7, local copies, waits for them, and re-layouts  17.1 us
    dot_general x8, matrix products, advance(): jnp.einsum('qd,kd->qk', queries, key_block, preferred_element_type=jnp.fl...  14 us
    reduce_sum x8, other arithmetic, advance(): new_sum = run_sum * factor + jnp.sum(weights, axis=1)  7.81 us
  transfers between devices with their start and end apart: 3, of which 3 were waited for; matrix products, arithmetic and copies ran while one was open for 1% of the time, Pallas kernels for 0%

profile of v2, /device:TPU:2, one launch (start us, length us, event | category | flops | bytes accessed | tf_op | source)
XLA Modules:
  0.0 359.7 jit_solution(9354017206300492714)
XLA Ops:
  6.5 6.1 %copy.17 = bf16[3,32,4096]{1,0,2:T(4,128)(2,1)} copy(bf16[3,32,4096]{2,1,0:T(8,128)(2,1)} %param.5) | data formatting | bytes 1572864 | tf_op args[0]
  12.6 6.2 %reshape.85 = bf16[32,2,6144]{2,1,0:T(2,128)(2,1)S(1)} reshape(bf16[4096,3,32]{2,1,0:T(4,128)(2,1)} %bitcast.48) | data formatting | bytes 1572864
  18.8 36.1 %all_to_all.20 = bf16[32,2,6144]{2,1,0:T(2,128)(2,1)S(1)} all-to-all(bf16[32,2,6144]{2,1,0:T(2,128)(2,1)S(1)} %reshape.85), channel_id=1, replica_groups=mesh['blk'=8,'tile'=32] {'tile'}, dimensions={0} | all-to-all | bytes 1572864 | tf_op jit(solution)/shard_map/all_to_all | solution.py:24
  54.9 4.8 %reshape.86 = bf16[4096,3,32]{2,1,0:T(4,128)(2,1)} reshape(bf16[32,2,6144]{2,1,0:T(2,128)(2,1)S(1)} %all_to_all.20) | data formatting | bytes 1572864
  59.8 4.2 %copy.22 = bf16[3,32,32,128]{3,2,1,0:T(8,128)(2,1)S(1)} copy(bf16[3,32,32,128]{1,0,3,2:T(4,128)(2,1)} %bitcast.47) | data formatting | bytes 1572864 | tf_op jit(solution)/shard_map/all_to_all | solution.py:24
  65.7 1.6 stack.3
  67.3 4.9 %all-to-all-start.1 = ((bf16[8,1024,128]{2,1,0:T(8,128)(2,1)}), bf16[8,1024,128]{2,1,0:T(8,128)(2,1)S(1)}, u32[]{:S(2)}, u32[]{:S(2)}) async-start(bf16[8,1024,128]{2,1,0:T(8,128)(2,1)} %stack.3), calls=%async_computation.1 | async-start | bytes 4194304 | tf_op jit(solution)/shard_map/all_to_all | solution.py:37
  72.4 1.8 copy.20
  74.1 30.8 %all-to-all-done.1 = bf16[8,1024,128]{2,1,0:T(8,128)(2,1)S(1)} async-done(((bf16[8,1024,128]{2,1,0:T(8,128)(2,1)}), bf16[8,1024,128]{2,1,0:T(8,128)(2,1)S(1)}, u32[]{:S(2)}, u32[]{:S(2)}) %all-to-all-start.1) | async-done | bytes 2097184 | tf_op jit(solution)/shard_map/all_to_all | solution.py:37
  104.9 19.4 %all-gather.2.cloned.1.call-done = bf16[8192,128]{1,0:T(8,128)(2,1)} async-done(((bf16[1024,128]{1,0:T(8,128)(2,1)}), bf16[8192,128]{1,0:T(8,128)(2,1)}) %all-gather.2.cloned.1.call-update) | async-done | bytes 2097168 | tf_op jit(solution)/shard_map/all_gather | solution.py:39
  124.3 58.0 %while.18 = (s32[]{:T(128)}, f32[1024]{0:T(1024)S(1)}, f32[1024]{0:T(1024)S(1)}, f32[1024,128]{1,0:T(8,128)}, s32[1024]{0:T(1024)S(1)}, /*index=5*/s32[8]{0:T(12...) while((s32[]{:T(128)}, f32[1024]{0:T(1024)S(1)}, ...), condition=%wide.region_5.6_spmd.clone, body=%wide.region_1.5_spmd.clone.sunk | while | flops 552039424 | bytes 18714904 | solution.py:66
  125.6 1.8 fusion.53
  127.4 1.0 fusion.54
  128.4 2.3 fusion.56
  132.9 1.8 fusion.53
  134.7 1.0 fusion.54
  135.7 2.3 fusion.56
  140.1 1.8 fusion.53
  141.9 1.0 fusion.54
  142.9 2.3 fusion.56
  147.4 1.8 fusion.53
  150.2 2.3 fusion.56
  154.6 1.8 fusion.53
  157.4 2.3 fusion.56
  161.9 1.8 fusion.53
  164.7 2.3 fusion.56
  169.1 1.8 fusion.53
  171.9 2.3 fusion.56
  176.4 1.8 fusion.53
  179.2 2.3 fusion.56
  182.3 6.6 %convolution_convert_fusion = bf16[1024,5120]{1,0:T(8,128)(2,1)} fusion(bf16[128,5120]{1,0:T(8,128)(2,1)S(1)} %copy-done, f32[1024,128]{1,0:T(8,128)} %get-tuple-element.169, f32[1024]{0:T(1024)S(1)} %get-tuple-element.170), kind=kOutput, calls=%fused_computation.49 | convolution fusion | flops 1347682304 | bytes 12324864 | tf_op jit(solution)/shard_map/dot_general | solution.py:70
  189.0 163.9 %reduce-scatter.2.cloned.1.call-done = bf16[32,5120]{1,0:T(8,128)(2,1)} async-done(((bf16[1024,5120]{1,0:T(8,128)(2,1)}), bf16[32,5120]{1,0:T(8,128)(2,1)}) %reduce-scatter.2.cloned.1.call-update) | async-done | bytes 327696 | tf_op jit(solution)/shard_map/reduce_scatter | solution.py:69
  (102 shorter events, 23.9 us)
Async XLA Ops:
  6.5 175.8 %copy-start = (bf16[128,5120]{1,0:T(8,128)(2,1)S(1)}, bf16[128,5120]{1,0:T(8,128)(2,1)}, u32[]{:S(2)}) copy-start(bf16[128,5120]{1,0:T(8,128)(2,1)} %param.7) | copy-start | bytes 3932164
  6.5 117.8 %all-gather.2.cloned.1.call-start = ((), (), s32[]{:S(2)}) async-start(), calls=%async_computation.3 | async-start | bytes 2359296 | tf_op jit(solution)/shard_map/all_gather | solution.py:39
  64.8 7.5 %copy-start.3 = (s32[16]{0:T(128)S(1)}, s32[16]{0:T(128)}, u32[]{:S(2)}) copy-start(s32[16]{0:T(128)} %param.6) | copy-start | bytes 196
  67.3 37.6 %all-to-all-start.1 = ((bf16[8,1024,128]{2,1,0:T(8,128)(2,1)}), bf16[8,1024,128]{2,1,0:T(8,128)(2,1)S(1)}, u32[]{:S(2)}, u32[]{:S(2)}) async-start(bf16[8,1024,128]{2,1,0:T(8,128)(2,1)} %stack.3), calls=%async_computation.1 | async-start | bytes 4194304 | tf_op jit(solution)/shard_map/all_to_all | solution.py:37
  72.2 280.7 %reduce-scatter.2.cloned.1.call-start = ((), (), s32[]{:S(2)}) async-start(), calls=%async_computation.4 | async-start | bytes 10813440 | tf_op jit(solution)/shard_map/reduce_scatter | solution.py:69
  125.6 2.8 copy-start.1
  130.7 0.8 copy-start.2
  132.9 2.8 copy-start.1
  138.0 0.8 copy-start.2
  140.1 2.8 copy-start.1
  145.2 0.8 copy-start.2
  147.4 2.8 copy-start.1
  152.5 0.8 copy-start.2
  154.6 2.8 copy-start.1
  159.7 0.8 copy-start.2
  161.9 2.8 copy-start.1
  167.0 0.8 copy-start.2
  169.1 2.8 copy-start.1
  174.2 0.8 copy-start.2
  176.4 2.8 copy-start.1
  181.5 0.8 copy-start.2
Sparse Core Ops, SparseCore 0:
  65.7 58.5 all-gather.1
  189.1 163.7 reduce-scatter.1
